TPU v7x, 256 devices: a whole 4x4x8 slice. The times are simulated.
256 devices in a mesh: px: 4 (over z_lo), py: 8 (over y, core), ch: 8 (over z_hi, x).
Axes of the slice: x: 4, y: 4, z: 8 (z_hi: 2, z_lo: 4; z = z_hi * 4 + z_lo), core: 2. Of those that a mesh axis runs over, the one named last changes fastest.
Arguments:
- features: bfloat16 [128, 12, 8, 4, 512], P('ch', None, 'py', 'px'), may hold values from -6 to 6
- cotangent: bfloat16 [128, 12, 8, 4, 512], P('ch', None, 'py', 'px'), may hold values from -6 to 6
- weight: bfloat16 [3, 3, 128, 128], replicated, may hold values from -0.1875 to 0.1875
- edge_table: int32 [12, 4, 3], replicated, may hold values from 0 to 11, as said below
- corner_table: int32 [12, 4, 2], replicated, may hold values from 0 to 11, as said below
Outputs:
- activation: bfloat16 [128, 12, 8, 4, 512], P('ch', None, 'py', 'px')
- input_grad: bfloat16 [128, 12, 8, 4, 512], P('ch', None, 'py', 'px')
Inputs may be any that keep to these rules, and one draw needn't show every extreme that they name: edge_table[f, e] = (g, s, r): beyond edge e of face f lie the pixels of side s of face g, in reverse order if r = 1; every side of every face is named exactly once, and if (f, e) names (g, s) then (g, s) names (f, e) with the same r. corner_table[f, c] = (h, q): corner c of face f takes corner pixel q of face h; in each corner column every face appears once, and each q appears 12 times.
All inputs are finite; a program needn't handle non-finite values.
Results may differ from a plain program's by a relative error of at most 0.0049.
Values may be sent and summed in bfloat16 or wider, within the bound.
A program may use at most 192 MiB of HBM per device.

v0:
```python
import jax
import jax.numpy as jnp
from jax import lax
from jax.sharding import PartitionSpec as P

RB = 32


def with_halo(array, sides, width):
    for axis, dim in sides:
        size, length = (lax.axis_size(axis), array.shape[dim])
        up = [(i, (i + 1) % size) for i in range(size - 1)]
        down = [(j, i) for i, j in up]
        last = lax.slice_in_dim(array, length - width, length, axis=dim)
        leading = lax.slice_in_dim(array, 0, width, axis=dim)
        before = lax.ppermute(last, axis, up)
        after = lax.ppermute(leading, axis, down)
        array = jnp.concatenate([before, array, after], axis=dim)
    return array


def edge_strips(lines, edge_table, corner_table):
    chan_count = lines.shape[0]
    face_count = lines.shape[1]
    side_len = lines.shape[3]
    flat_lines = lines.reshape(chan_count, face_count * 4, side_len)
    pixels = jnp.stack(
        [lines[:, :, 0, 0], lines[:, :, 0, -1], lines[:, :, 1, 0], lines[:, :, 1, -1]], axis=2
    ).reshape(chan_count, face_count * 4)
    corner_index = corner_table[:, :, 0] * 4 + corner_table[:, :, 1]
    corner_vals = jnp.take(pixels, corner_index, axis=1)
    strips = []
    for edge_num, start_corner, end_corner in ((0, 0, 1), (1, 2, 3), (2, 0, 2), (3, 1, 3)):
        source_row = edge_table[:, edge_num, 0] * 4 + edge_table[:, edge_num, 1]
        strip_line = jnp.take(flat_lines, source_row, axis=1)
        flipped = (edge_table[:, edge_num, 2] == 1)[None, :, None]
        strip_line = jnp.where(flipped, strip_line[:, :, ::-1], strip_line)
        strips.append(
            jnp.concatenate(
                [
                    corner_vals[:, :, start_corner : start_corner + 1],
                    strip_line,
                    corner_vals[:, :, end_corner : end_corner + 1],
                ],
                axis=2,
            )
        )
    return strips


def face_lines_of(field, row_pos, col_pos, px_count, py_count):
    chan_block = field.shape[0]
    face_count = field.shape[1]
    col_len = field.shape[2]
    row_len = field.shape[3]
    side_len = row_len * px_count
    blank = jnp.zeros((chan_block, face_count, side_len), jnp.float32)

    def placed(values, offset, active):
        return jnp.where(
            active,
            lax.dynamic_update_slice_in_dim(blank, values.astype(jnp.float32), offset, 2),
            0.0,
        )

    contrib = jnp.stack(
        [
            placed(field[:, :, 0, :], row_pos * row_len, col_pos == 0),
            placed(field[:, :, -1, :], row_pos * row_len, col_pos == py_count - 1),
            placed(field[:, :, :, 0], col_pos * col_len, row_pos == 0),
            placed(field[:, :, :, -1], col_pos * col_len, row_pos == px_count - 1),
        ],
        axis=2,
    )
    return lax.psum(contrib.astype(jnp.bfloat16), ("px", "py"))


def pad_field(field, edge_table, corner_table):
    col_len = field.shape[2]
    row_len = field.shape[3]
    row_pos = lax.axis_index("px")
    col_pos = lax.axis_index("py")
    px_count = lax.axis_size("px")
    py_count = lax.axis_size("py")
    padded = with_halo(field, (("px", 3), ("py", 2)), 1)
    lines = face_lines_of(field, row_pos, col_pos, px_count, py_count)
    strips = edge_strips(lines, edge_table, corner_table)
    top_row = lax.dynamic_slice_in_dim(strips[0], row_pos * row_len, row_len + 2, 2)
    bottom_row = lax.dynamic_slice_in_dim(strips[1], row_pos * row_len, row_len + 2, 2)
    left_col = lax.dynamic_slice_in_dim(strips[2], col_pos * col_len, col_len + 2, 2)
    right_col = lax.dynamic_slice_in_dim(strips[3], col_pos * col_len, col_len + 2, 2)
    padded = padded.at[:, :, 0, :].set(jnp.where(col_pos == 0, top_row, padded[:, :, 0, :]))
    padded = padded.at[:, :, -1, :].set(
        jnp.where(col_pos == py_count - 1, bottom_row, padded[:, :, -1, :])
    )
    padded = padded.at[:, :, :, 0].set(jnp.where(row_pos == 0, left_col, padded[:, :, :, 0]))
    padded = padded.at[:, :, :, -1].set(
        jnp.where(row_pos == px_count - 1, right_col, padded[:, :, :, -1])
    )
    return padded


def forward_taps(padded, taps, out_cols, out_rows):
    summed = None
    for tap_row in range(3):
        for tap_col in range(3):
            window = padded[:, :, tap_row : tap_row + out_cols, tap_col : tap_col + out_rows]
            term_val = jnp.einsum(
                "oc,cfab->ofab", taps[tap_row, tap_col], window, preferred_element_type=jnp.float32
            )
            summed = term_val if summed is None else summed + term_val
    return summed


def backward_taps(padded, taps, out_cols, out_rows):
    summed = None
    for tap_row in range(3):
        for tap_col in range(3):
            window = padded[
                :, :, 2 - tap_row : 2 - tap_row + out_cols, 2 - tap_col : 2 - tap_col + out_rows
            ]
            term_val = jnp.einsum(
                "oc,ofab->cfab", taps[tap_row, tap_col], window, preferred_element_type=jnp.float32
            )
            summed = term_val if summed is None else summed + term_val
    return summed


def gate_outputs(preact, cotangent):
    sigmoid_val = jax.nn.sigmoid(preact)
    activation = (preact * sigmoid_val).astype(jnp.bfloat16)
    gated = (
        cotangent.astype(jnp.float32) * sigmoid_val * (1.0 + preact * (1.0 - sigmoid_val))
    ).astype(jnp.bfloat16)
    return (activation, gated)


def local(features, cotangent, weight, edge_table, corner_table):
    chan_block = features.shape[0]
    face_count = features.shape[1]
    tile_len = features.shape[4]
    row_len = RB
    col_len = tile_len // row_len
    features = features.reshape(chan_block, face_count, col_len, row_len)
    cotangent = cotangent.reshape(chan_block, face_count, col_len, row_len)
    ch_pos = lax.axis_index("ch")
    feat_pad = pad_field(features, edge_table, corner_table)
    own_taps = lax.dynamic_slice_in_dim(weight, ch_pos * chan_block, chan_block, 2)
    piece_taps = own_taps
    preact = forward_taps(
        lax.all_gather(feat_pad, "ch", axis=0, tiled=True), piece_taps, col_len, row_len
    )
    activation, gated = gate_outputs(preact, cotangent)
    grad_pad = pad_field(gated, edge_table, corner_table)
    input_taps = lax.dynamic_slice_in_dim(weight, ch_pos * chan_block, chan_block, 3)
    piece_taps = input_taps
    input_grad = backward_taps(
        lax.all_gather(grad_pad, "ch", axis=0, tiled=True), piece_taps, col_len, row_len
    ).astype(jnp.bfloat16)
    out_shape = (chan_block, face_count, 1, 1, tile_len)
    return (activation.reshape(out_shape), input_grad.reshape(out_shape))


def solution(mesh):
    return jax.shard_map(
        local,
        mesh=mesh,
        in_specs=(P("ch", None, "py", "px", None), P("ch", None, "py", "px", None), P(), P(), P()),
        out_specs=(P("ch", None, "py", "px", None), P("ch", None, "py", "px", None)),
        check_vma=False,
    )
```

profile of v0, /device:TPU:8, one launch (start us, length us, event | category | flops | bytes accessed | tf_op | source)
XLA Modules:
  0.0 1055.1 jit_solution(10775510683861696942)
XLA Ops:
  11.2 3.0 copy.696
  16.1 2.7 select_n.196
  18.7 2.7 select_n.200
  23.1 2.6 copy.698
  27.0 7.1 collective-permute-start
  45.5 3.9 collective-permute-start.3
  53.1 254.8 %all-reduce.3.cloned.1.call-done = bf16[16,12,4,128]{1,0,3,2:T(8,128)(2,1)} async-done(((bf16[16,12,4,128]{1,0,3,2:T(8,128)(2,1)}), bf16[16,12,4,128]{1,0,3,2:T(8,128)(2,1)}) %all-reduce.3.cloned.1.call-update) | async-done | bytes 196624 | tf_op jit(solution)/shard_map/psum | solution.py:75
  307.9 3.0 copy.702
  318.9 3.8 scatter.30
  326.8 18.3 %scatter.31 = bf16[16,12,18,34]{3,0,2,1:T(8,128)(2,1)S(1)} dynamic-update-slice(bf16[16,12,18,34]{3,0,2,1:T(8,128)(2,1)S(1)} %scatter.30, bf16[16,12,18,1]{3,0,2,1:T(8,128)(2,1)S(1)} %copy.707, s32[]{:T(128)} %constant.235.clone.1, s32[]{:T(128)} %constant.235.clone.1, s32[]{:T(128)} %constant.235.clone.1, s32[]{:T(128)} %constant.249.clone.1) | dynamic-update-slice | bytes 13828 | tf_op jit(solution)/shard_map/scatter | solution.py:97
  347.9 162.8 %all-gather.3.cloned.1.call-done = bf16[128,12,18,34]{3,0,2,1:T(8,128)(2,1)} async-done(((bf16[16,12,18,34]{3,0,2,1:T(8,128)(2,1)}), bf16[128,12,18,34]{3,0,2,1:T(8,128)(2,1)}) %all-gather.3.cloned.1.call-update) | async-done | bytes 1880080 | tf_op jit(solution)/shard_map/all_gather | solution.py:151
  510.7 4.7 fusion.20
  526.6 2.6 fusion.37
  531.6 2.3 copy.725
  536.3 2.2 collective-permute-start.4
  545.7 2.6 copy.727
  553.0 3.9 collective-permute-start.7
  559.2 266.2 %all-reduce.5.cloned.1.call-done = bf16[16,12,4,128]{1,0,3,2:T(8,128)(2,1)} async-done(((bf16[16,12,4,128]{1,0,3,2:T(8,128)(2,1)}), bf16[16,12,4,128]{1,0,3,2:T(8,128)(2,1)}) %all-reduce.5.cloned.1.call-update) | async-done | bytes 196624 | tf_op jit(solution)/shard_map/psum | solution.py:75
  825.4 3.0 copy.731
  837.1 3.8 scatter.36
  844.2 18.6 %scatter.39 = bf16[16,12,18,34]{3,0,2,1:T(8,128)(2,1)S(1)} dynamic-update-slice(bf16[16,12,18,34]{3,0,2,1:T(8,128)(2,1)S(1)} %scatter.36, bf16[16,12,18,1]{3,0,2,1:T(8,128)(2,1)S(1)} %copy.735, s32[]{:T(128)} %constant.235.clone.1, s32[]{:T(128)} %constant.235.clone.1, s32[]{:T(128)} %constant.235.clone.1, s32[]{:T(128)} %constant.249.clone.1) | dynamic-update-slice | bytes 13828 | tf_op jit(solution)/shard_map/scatter | solution.py:97
  865.5 162.9 %all-gather.5.cloned.1.call-done = bf16[128,12,18,34]{3,0,2,1:T(8,128)(2,1)} async-done(((bf16[16,12,18,34]{3,0,2,1:T(8,128)(2,1)}), bf16[128,12,18,34]{3,0,2,1:T(8,128)(2,1)}) %all-gather.5.cloned.1.call-update) | async-done | bytes 1880080 | tf_op jit(solution)/shard_map/all_gather | solution.py:158
  1028.4 4.8 fusion.2
  1044.1 2.3 add_convert_fusion
  (209 shorter events, 95.3 us)
Async XLA Ops:
  7.2 503.6 %copy-start = (bf16[3,3,128,128]{3,2,1,0:T(8,128)(2,1)S(1)}, bf16[3,3,128,128]{3,2,1,0:T(8,128)(2,1)}, u32[]{:S(2)}) copy-start(bf16[3,3,128,128]{3,2,1,0:T(8,128)(2,1)} %param.27) | copy-start | bytes 884740
  7.2 300.8 %all-reduce.3.cloned.1.call-start = ((), (), s32[]{:S(2)}) async-start(), calls=%async_computation | async-start | bytes 4194304 | tf_op jit(solution)/shard_map/psum | solution.py:75
  25.7 10.9 %copy-start.17 = (s32[12,4,3]{0,1,2:T(4,128)S(1)}, s32[12,4,3]{0,1,2:T(4,128)}, u32[]{:S(2)}) copy-start(s32[12,4,3]{0,1,2:T(4,128)} %param.28) | copy-start | bytes 1732
  25.7 12.0 %copy-start.26 = (s32[12,4,2]{0,2,1:T(2,128)S(1)}, s32[12,4,2]{0,2,1:T(2,128)}, u32[]{:S(2)}) copy-start(s32[12,4,2]{0,2,1:T(2,128)} %param.29) | copy-start | bytes 1156
  25.7 485.0 %all-gather.3.cloned.1.call-start = ((), (), s32[]{:S(2)}) async-start(), calls=%async_computation.1 | async-start | bytes 7962624 | tf_op jit(solution)/shard_map/all_gather | solution.py:151
  27.0 12.3 %collective-permute-start = (bf16[16,12,16,1]{2,0,3,1:T(8,128)(2,1)S(1)}, bf16[16,12,16,1]{2,0,3,1:T(8,128)(2,1)S(1)}, u32[]{:S(2)}, u32[]{:S(2)}) collective-permute-start(bf16[16,12,16,1]{2,0,3,1:T(8,128)(2,1)S(1)} %copy.684), channel_id=1, source_target_pairs={{0,64},{64,128},{128,192},{1,65},{65,129},{129,193},{2,66},{66,130... | collective-permute-start | bytes 18440 | tf_op jit(solution)/shard_map/ppermute | solution.py:16
  35.3 6.0 collective-permute-start.1
  43.6 5.9 collective-permute-start.2
  45.5 5.4 collective-permute-start.3
  53.1 258.7 %copy-start.15 = (pred[12]{0:T(512)(128)(4,1)S(1)}, pred[12]{0:T(512)(128)(4,1)}, u32[]{:S(2)}) copy-start(pred[12]{0:T(512)(128)(4,1)} %get-tuple-element.166) | copy-start | bytes 40
  53.1 259.6 %copy-start.13 = (pred[12]{0:T(512)(128)(4,1)S(1)}, pred[12]{0:T(512)(128)(4,1)}, u32[]{:S(2)}) copy-start(pred[12]{0:T(512)(128)(4,1)} %get-tuple-element.164) | copy-start | bytes 40
  346.1 479.3 %all-reduce.5.cloned.1.call-start = ((), (), s32[]{:S(2)}) async-start(), calls=%async_computation.2 | async-start | bytes 4194304 | tf_op jit(solution)/shard_map/psum | solution.py:75
  535.1 9.9 copy-start.7
  535.1 10.2 copy-start.6
  536.3 12.1 %collective-permute-start.4 = (bf16[16,12,16,1]{2,0,3,1:T(8,128)(2,1)S(1)}, bf16[16,12,16,1]{2,0,3,1:T(8,128)(2,1)S(1)}, u32[]{:S(2)}, u32[]{:S(2)}) collective-permute-start(bf16[16,12,16,1]{2,0,3,1:T(8,128)(2,1)S(1)} %copy.720), channel_id=1, source_target_pairs={{0,64},{64,128},{128,192},{1,65},{65,129},{129,193},{2,66},{66,130... | collective-permute-start | bytes 18440 | tf_op jit(solution)/shard_map/ppermute | solution.py:16
  539.8 9.9 collective-permute-start.5
  548.4 480.1 %all-gather.5.cloned.1.call-start = ((), (), s32[]{:S(2)}) async-start(), calls=%async_computation.3 | async-start | bytes 7962624 | tf_op jit(solution)/shard_map/all_gather | solution.py:158
  551.1 5.8 collective-permute-start.6
  553.0 5.4 collective-permute-start.7
  559.1 272.2 %copy-start.16 = (pred[12]{0:T(512)(128)(4,1)S(1)}, pred[12]{0:T(512)(128)(4,1)}, u32[]{:S(2)}) copy-start(pred[12]{0:T(512)(128)(4,1)} %get-tuple-element.166) | copy-start | bytes 40
  559.2 272.4 %copy-start.25 = (pred[12]{0:T(512)(128)(4,1)S(1)}, pred[12]{0:T(512)(128)(4,1)}, u32[]{:S(2)}) copy-start(pred[12]{0:T(512)(128)(4,1)} %get-tuple-element.162) | copy-start | bytes 40
  559.2 272.5 %copy-start.14 = (pred[12]{0:T(512)(128)(4,1)S(1)}, pred[12]{0:T(512)(128)(4,1)}, u32[]{:S(2)}) copy-start(pred[12]{0:T(512)(128)(4,1)} %get-tuple-element.164) | copy-start | bytes 40
  559.2 272.7 %copy-start.23 = (pred[12]{0:T(512)(128)(4,1)S(1)}, pred[12]{0:T(512)(128)(4,1)}, u32[]{:S(2)}) copy-start(pred[12]{0:T(512)(128)(4,1)} %get-tuple-element.161) | copy-start | bytes 40
  842.9 20.9 %copy-start.5 = (bf16[16,12,16,32]{3,0,2,1:T(8,128)(2,1)S(1)}, bf16[16,12,16,32]{3,0,2,1:T(8,128)(2,1)}, u32[]{:S(2)}) copy-start(bf16[16,12,16,32]{3,0,2,1:T(8,128)(2,1)} %get-tuple-element.139) | copy-start | bytes 589828
  (15 other events, 48.2 us)
Sparse Core Ops, SparseCore 0:
  25.8 282.0 all-reduce.2
  346.2 164.4 all-gather.2
  548.5 276.8 all-reduce.4
  863.9 164.4 all-gather.4
where the time goes:
time: 1060 us
  waiting for transfers between devices  850 us (80%)
  local copies, waits for them, and re-layouts  117 us (11%)
  matrix products  36.3 us (3%)
  starting transfers between devices  24 us (2%)
  between operations  15.2 us (1%)
  other arithmetic  12.9 us (1%)
    psum x2, waiting for transfers between devices, face_lines_of(): return lax.psum(contrib.astype(jnp.bfloat16), ('px', 'py'))  521 us
    all_gather x1, waiting for transfers between devices, local(): lax.all_gather(grad_pad, 'ch', axis=0, tiled=True)  163 us
    all_gather x1, waiting for transfers between devices, local(): lax.all_gather(feat_pad, 'ch', axis=0, tiled=True)  163 us
    scatter x2, local copies, waits for them, and re-layouts, pad_field(): padded.at[:, :, :, -1]  36.9 us
  transfers between devices with their start and end apart: 12, of which 7 were waited for; matrix products, arithmetic and copies ran while one was open for 2% of the time, Pallas kernels for 0%

commit v1 on v0

--- a/solution.py
+++ b/solution.py
@@ -1,9 +1,18 @@
+import functools
 import jax
 import jax.numpy as jnp
 from jax import lax
 from jax.sharding import PartitionSpec as P
 
 RB = 32
+
+
+def spot_switch(unit, axis_tag, shard_axis):
+    newest = lax.psum(unit, axis_tag)
+    return lax.psum(newest, shard_axis)
+
+
+connect_the_terms = functools.partial(spot_switch, axis_tag="py", shard_axis="px")
 
 
 def with_halo(array, sides, width):
@@ -72,7 +81,7 @@
         ],
         axis=2,
     )
-    return lax.psum(contrib.astype(jnp.bfloat16), ("px", "py"))
+    return connect_the_terms(contrib.astype(jnp.bfloat16))
 
 
 def pad_field(field, edge_table, corner_table):

time: 1060 us -> 838 us (0.79)
  waiting for transfers between devices: 850 us -> 619 us
    psum x2 -> x4, waiting for transfers between devices: 521 us -> 297 us  [the longest x2 194 us: spot_switch(): return lax.psum(newest, shard_axis)]
  transfers between devices with their start and end apart: 12 -> 14, of which waited for: 7 -> 9; matrix products, arithmetic and copies ran while one was open for 2% -> 2% of each run, Pallas kernels for 0% -> 0%
where the time goes in v1:
time: 838 us; the launch traced here: 829 us
  waiting for transfers between devices  619 us (74%)
  local copies, waits for them, and re-layouts  118 us (14%)
  matrix products  36.3 us (4%)
  starting transfers between devices  27.3 us (3%)
  between operations  15.6 us (2%)
  other arithmetic  12.9 us (2%)
    psum x2, waiting for transfers between devices, spot_switch(): return lax.psum(newest, shard_axis)  194 us
    all_gather x1, waiting for transfers between devices, local(): lax.all_gather(feat_pad, 'ch', axis=0, tiled=True)  159 us
    all_gather x1, waiting for transfers between devices, local(): lax.all_gather(grad_pad, 'ch', axis=0, tiled=True)  157 us
    psum x2, waiting for transfers between devices, spot_switch(): newest = lax.psum(unit, axis_tag)  103 us
    scatter x2, local copies, waits for them, and re-layouts, pad_field(): padded.at[:, :, :, -1]  36.9 us
    select_n x12, local copies, waits for them, and re-layouts, placed(): jnp.where(active, lax.dynamic_update_slice_in_dim(blank, values.astype(jn...  20.3 us
    dot_general x9, matrix products, forward_taps(): jnp.einsum('oc,cfab->ofab', taps[tap_row, tap_col], window, preferred_ele...  18.4 us
    dot_general x9, matrix products, backward_taps(): jnp.einsum('oc,ofab->cfab', taps[tap_row, tap_col], window, preferred_ele...  17.9 us
  transfers between devices with their start and end apart: 14, of which 9 were waited for; matrix products, arithmetic and copies ran while one was open for 2% of the time, Pallas kernels for 0%

profile of v1, /device:TPU:8, one launch (start us, length us, event | category | flops | bytes accessed | tf_op | source)
XLA Modules:
  0.0 829.4 jit_solution(11760332068274076259)
XLA Ops:
  11.2 3.0 copy.696
  16.0 2.7 select_n.196
  18.7 2.7 select_n.200
  23.0 2.6 copy.698
  27.0 7.1 collective-permute-start
  45.5 3.6 collective-permute-start.3
  49.1 50.8 %all-reduce.5.cloned.1.call-done = bf16[16,12,4,128]{1,0,3,2:T(8,128)(2,1)} async-done(((bf16[16,12,4,128]{1,0,3,2:T(8,128)(2,1)}), bf16[16,12,4,128]{1,0,3,2:T(8,128)(2,1)}) %all-reduce.5.cloned.1.call-update) | async-done | bytes 196624 | tf_op jit(solution)/shard_map/psum | solution.py:11
  102.7 99.9 %all-reduce.7.cloned.1.call-done = bf16[16,12,4,128]{1,0,3,2:T(8,128)(2,1)} async-done(((bf16[16,12,4,128]{1,0,3,2:T(8,128)(2,1)}), bf16[16,12,4,128]{1,0,3,2:T(8,128)(2,1)}) %all-reduce.7.cloned.1.call-update) | async-done | bytes 196624 | tf_op jit(solution)/shard_map/psum | solution.py:12
  202.6 3.0 copy.702
  213.6 3.8 scatter.30
  221.4 18.3 %scatter.31 = bf16[16,12,18,34]{3,0,2,1:T(8,128)(2,1)S(1)} dynamic-update-slice(bf16[16,12,18,34]{3,0,2,1:T(8,128)(2,1)S(1)} %scatter.30, bf16[16,12,18,1]{3,0,2,1:T(8,128)(2,1)S(1)} %copy.707, s32[]{:T(128)} %constant.235.clone.1, s32[]{:T(128)} %constant.235.clone.1, s32[]{:T(128)} %constant.235.clone.1, s32[]{:T(128)} %constant.249.clone.1) | dynamic-update-slice | bytes 13828 | tf_op jit(solution)/shard_map/scatter | solution.py:106
  241.6 159.3 %all-gather.3.cloned.1.call-done = bf16[128,12,18,34]{3,0,2,1:T(8,128)(2,1)} async-done(((bf16[16,12,18,34]{3,0,2,1:T(8,128)(2,1)}), bf16[128,12,18,34]{3,0,2,1:T(8,128)(2,1)}) %all-gather.3.cloned.1.call-update) | async-done | bytes 1880080 | tf_op jit(solution)/shard_map/all_gather | solution.py:160
  400.9 4.7 fusion.20
  431.4 2.6 copy.727
  435.3 5.4 collective-permute-start.4
  444.6 3.4 collective-permute-done.5
  449.3 52.0 %all-reduce.9.cloned.1.call-done = bf16[16,12,4,128]{1,0,3,2:T(8,128)(2,1)} async-done(((bf16[16,12,4,128]{1,0,3,2:T(8,128)(2,1)}), bf16[16,12,4,128]{1,0,3,2:T(8,128)(2,1)}) %all-reduce.9.cloned.1.call-update) | async-done | bytes 196624 | tf_op jit(solution)/shard_map/psum | solution.py:11
  503.4 3.9 collective-permute-start.7
  509.5 94.4 %all-reduce.11.cloned.1.call-done = bf16[16,12,4,128]{1,0,3,2:T(8,128)(2,1)} async-done(((bf16[16,12,4,128]{1,0,3,2:T(8,128)(2,1)}), bf16[16,12,4,128]{1,0,3,2:T(8,128)(2,1)}) %all-reduce.11.cloned.1.call-update) | async-done | bytes 196624 | tf_op jit(solution)/shard_map/psum | solution.py:12
  603.9 3.0 copy.731
  615.6 3.8 scatter.36
  622.7 18.6 %scatter.39 = bf16[16,12,18,34]{3,0,2,1:T(8,128)(2,1)S(1)} dynamic-update-slice(bf16[16,12,18,34]{3,0,2,1:T(8,128)(2,1)S(1)} %scatter.36, bf16[16,12,18,1]{3,0,2,1:T(8,128)(2,1)S(1)} %copy.735, s32[]{:T(128)} %constant.235.clone.1, s32[]{:T(128)} %constant.235.clone.1, s32[]{:T(128)} %constant.235.clone.1, s32[]{:T(128)} %constant.249.clone.1) | dynamic-update-slice | bytes 13828 | tf_op jit(solution)/shard_map/scatter | solution.py:106
  645.1 157.4 %all-gather.5.cloned.1.call-done = bf16[128,12,18,34]{3,0,2,1:T(8,128)(2,1)} async-done(((bf16[16,12,18,34]{3,0,2,1:T(8,128)(2,1)}), bf16[128,12,18,34]{3,0,2,1:T(8,128)(2,1)}) %all-gather.5.cloned.1.call-update) | async-done | bytes 1880080 | tf_op jit(solution)/shard_map/all_gather | solution.py:167
  802.5 4.8 fusion.2
  (211 shorter events, 103.0 us)
Async XLA Ops:
  7.2 393.8 %copy-start = (bf16[3,3,128,128]{3,2,1,0:T(8,128)(2,1)S(1)}, bf16[3,3,128,128]{3,2,1,0:T(8,128)(2,1)}, u32[]{:S(2)}) copy-start(bf16[3,3,128,128]{3,2,1,0:T(8,128)(2,1)} %param.27) | copy-start | bytes 884740
  7.2 92.8 %all-reduce.5.cloned.1.call-start = ((), (), s32[]{:S(2)}) async-start(), calls=%async_computation | async-start | bytes 4194304 | tf_op jit(solution)/shard_map/psum | solution.py:11
  25.7 12.1 %copy-start.24 = (s32[12,4,2]{0,2,1:T(2,128)S(1)}, s32[12,4,2]{0,2,1:T(2,128)}, u32[]{:S(2)}) copy-start(s32[12,4,2]{0,2,1:T(2,128)} %param.29) | copy-start | bytes 1156
  25.7 176.9 %all-reduce.7.cloned.1.call-start = ((), (), s32[]{:S(2)}) async-start(), calls=%async_computation.1 | async-start | bytes 4194304 | tf_op jit(solution)/shard_map/psum | solution.py:12
  27.0 12.4 %collective-permute-start = (bf16[16,12,16,1]{2,0,3,1:T(8,128)(2,1)S(1)}, bf16[16,12,16,1]{2,0,3,1:T(8,128)(2,1)S(1)}, u32[]{:S(2)}, u32[]{:S(2)}) collective-permute-start(bf16[16,12,16,1]{2,0,3,1:T(8,128)(2,1)S(1)} %copy.684), channel_id=1, source_target_pairs={{0,64},{64,128},{128,192},{1,65},{65,129},{129,193},{2,66},{66,130... | collective-permute-start | bytes 18440 | tf_op jit(solution)/shard_map/ppermute | solution.py:25
  35.3 6.0 collective-permute-start.1
  43.6 56.8 %collective-permute-start.2 = (bf16[16,12,1,34]{3,0,1,2:T(8,128)(2,1)S(1)}, bf16[16,12,1,34]{3,0,1,2:T(8,128)(2,1)S(1)}, u32[]{:S(2)}, u32[]{:S(2)}) collective-permute-start(bf16[16,12,1,34]{3,0,1,2:T(8,128)(2,1)S(1)} %get-tuple-element.148), channel_id=1, source_target_pairs={{0,8},{8,16},{16,24},{24,32},{32,40},{40,48},{48,56},{1,9},{9,17},... | collective-permute-start | bytes 39176 | tf_op jit(solution)/shard_map/ppermute | solution.py:25
  45.5 54.9 %collective-permute-start.3 = (bf16[16,12,1,34]{3,0,1,2:T(8,128)(2,1)S(1)}, bf16[16,12,1,34]{3,0,1,2:T(8,128)(2,1)S(1)}, u32[]{:S(2)}, u32[]{:S(2)}) collective-permute-start(bf16[16,12,1,34]{3,0,1,2:T(8,128)(2,1)S(1)} %get-tuple-element.149), channel_id=1, source_target_pairs={{8,0},{16,8},{24,16},{32,24},{40,32},{48,40},{56,48},{9,1},{17,9},... | collective-permute-start | bytes 39176 | tf_op jit(solution)/shard_map/ppermute | solution.py:26
  100.0 300.9 %all-gather.3.cloned.1.call-start = ((), (), s32[]{:S(2)}) async-start(), calls=%async_computation.2 | async-start | bytes 7962624 | tf_op jit(solution)/shard_map/all_gather | solution.py:160
  102.6 103.9 %copy-start.13 = (pred[12]{0:T(512)(128)(4,1)S(1)}, pred[12]{0:T(512)(128)(4,1)}, u32[]{:S(2)}) copy-start(pred[12]{0:T(512)(128)(4,1)} %get-tuple-element.166) | copy-start | bytes 40
  102.6 104.7 %copy-start.11 = (pred[12]{0:T(512)(128)(4,1)S(1)}, pred[12]{0:T(512)(128)(4,1)}, u32[]{:S(2)}) copy-start(pred[12]{0:T(512)(128)(4,1)} %get-tuple-element.164) | copy-start | bytes 40
  102.6 107.6 %copy-start.18 = (pred[12]{0:T(512)(128)(4,1)S(1)}, pred[12]{0:T(512)(128)(4,1)}, u32[]{:S(2)}) copy-start(pred[12]{0:T(512)(128)(4,1)} %get-tuple-element.163) | copy-start | bytes 40
  220.1 21.1 %copy-start.5 = (bf16[16,12,1,1,512]{4,0,3,2,1:T(8,128)(2,1)S(1)}, bf16[16,12,1,1,512]{4,0,3,2,1:T(8,128)(2,1)}, u32[]{:S(2)}) copy-start(bf16[16,12,1,1,512]{4,0,3,2,1:T(8,128)(2,1)} %param.26) | copy-start | bytes 589828
  240.8 260.4 %all-reduce.9.cloned.1.call-start = ((), (), s32[]{:S(2)}) async-start(), calls=%async_computation.3 | async-start | bytes 4194304 | tf_op jit(solution)/shard_map/psum | solution.py:11
  434.1 169.8 %all-reduce.11.cloned.1.call-start = ((), (), s32[]{:S(2)}) async-start(), calls=%async_computation.4 | async-start | bytes 4194304 | tf_op jit(solution)/shard_map/psum | solution.py:12
  435.3 8.0 collective-permute-start.4
  442.0 6.0 collective-permute-start.5
  501.2 301.2 %all-gather.5.cloned.1.call-start = ((), (), s32[]{:S(2)}) async-start(), calls=%async_computation.5 | async-start | bytes 7962624 | tf_op jit(solution)/shard_map/all_gather | solution.py:167
  501.4 5.8 collective-permute-start.6
  503.4 5.4 collective-permute-start.7
  509.5 100.4 %copy-start.14 = (pred[12]{0:T(512)(128)(4,1)S(1)}, pred[12]{0:T(512)(128)(4,1)}, u32[]{:S(2)}) copy-start(pred[12]{0:T(512)(128)(4,1)} %get-tuple-element.166) | copy-start | bytes 40
  509.5 100.6 %copy-start.23 = (pred[12]{0:T(512)(128)(4,1)S(1)}, pred[12]{0:T(512)(128)(4,1)}, u32[]{:S(2)}) copy-start(pred[12]{0:T(512)(128)(4,1)} %get-tuple-element.162) | copy-start | bytes 40
  509.5 100.7 %copy-start.12 = (pred[12]{0:T(512)(128)(4,1)S(1)}, pred[12]{0:T(512)(128)(4,1)}, u32[]{:S(2)}) copy-start(pred[12]{0:T(512)(128)(4,1)} %get-tuple-element.164) | copy-start | bytes 40
  509.5 100.9 %copy-start.21 = (pred[12]{0:T(512)(128)(4,1)S(1)}, pred[12]{0:T(512)(128)(4,1)}, u32[]{:S(2)}) copy-start(pred[12]{0:T(512)(128)(4,1)} %get-tuple-element.161) | copy-start | bytes 40
  (15 other events, 54.7 us)
Sparse Core Ops, SparseCore 0:
  25.8 74.1 all-reduce.4
  102.6 99.9 all-reduce.6
  240.9 159.9 all-gather.2
  434.2 66.9 all-reduce.8
  503.9 99.9 all-reduce.10
  642.4 159.9 all-gather.4
